TPU v7x, 128 devices: a whole 4x4x4 slice. The times are simulated.
128 devices in a mesh: row: 16 (over y, x_lo, core), col: 8 (over z, x_hi).
Axes of the slice: x: 4 (x_hi: 2, x_lo: 2; x = x_hi * 2 + x_lo), y: 4, z: 4, core: 2. Of those that a mesh axis runs over, the one named last changes fastest.
Arguments:
- tokens: bfloat16 [2048, 16384], P('col', 'row'), may hold values from -160 to 160
- norm_gain: bfloat16 [16384], P('row'), may hold values from 0.5 to 1.5
- gate_weight: bfloat16 [16384, 26624], P('row', 'col'), may hold values from -0.046875 to 0.046875
Outputs:
- gate_out: float32 [2048, 26624], P('row', 'col')
- token_peak: float32 [2048], P('col')
All inputs are finite; a program needn't handle non-finite values.
Results may differ from a plain program's by a relative error of at most 0.008.
Values may be sent and summed in bfloat16 or wider, within the bound.
No kernel may reach another device: no remote copies, remote signals or barrier semaphores. Data moves between devices by JAX's collectives and lax.ppermute only.
A program may use at most 128 MiB of HBM per device.

v0:
```python
import jax
import jax.numpy as jnp
from jax import lax
from jax.sharding import PartitionSpec as P

D = 16384


def copy_for_each(shard, axis):
    count = lax.axis_size(axis)
    return lax.all_to_all(
        jnp.broadcast_to(shard[None], (count, *shard.shape)), axis, 0, 0, tiled=True
    )


def all_in_one(shard, axis):
    leaves = jax.tree.leaves(shard)
    turns = sorted(range(len(leaves)), key=lambda k: -leaves[k].size)
    width = (1, *leaves[turns[0]].shape)[-1]
    lines = [
        jnp.pad(leaves[k].reshape(-1), (0, -leaves[k].size % width)).reshape(-1, width)
        for k in turns
    ]
    both, at, found = (copy_for_each(jnp.concatenate(lines), axis), 0, {})
    for k, line in zip(turns, lines):
        slab = both[:, at : at + len(line)].reshape(len(both), -1)
        found[k] = slab[:, : leaves[k].size].reshape(-1, *leaves[k].shape)
        at += len(line)
    numbers = iter(range(len(leaves)))
    return jax.tree.map(lambda _: found[next(numbers)], shard)


def folded_in_pairs(pieces, combine):
    while len(jax.tree.leaves(pieces)[0]) > 1:
        pieces = jax.vmap(combine)(
            *(jax.tree.map(lambda part: part[side::2], pieces) for side in (0, 1))
        )
    return jax.tree.map(lambda part: part[0], pieces)


def joined_all(shard, axis, combine):
    pieces = all_in_one(shard, axis)
    return folded_in_pairs(pieces, combine)


def combine_stats(first, second):
    return (first[0] + second[0], jnp.maximum(first[1], second[1]))


def shards(tokens, norm_gain, gate_weight):
    values = tokens.astype(jnp.float32)
    gain = norm_gain.astype(jnp.float32)[None, :]
    squares = jnp.sum(values * values, axis=1)
    weighted = jnp.max(jnp.abs(values * gain), axis=1)
    square_sum, peak = joined_all((squares, weighted), "row", combine_stats)
    inverse = lax.rsqrt(square_sum / D + 1e-05)
    normed = values * inverse[:, None] * gain
    token_peak = peak * inverse
    scale = ((token_peak + 1e-06) / 448.0).astype(jnp.bfloat16)
    quant = (normed / scale.astype(jnp.float32)[:, None]).astype(jnp.bfloat16)
    quant_full, scale_full = (
        lax.all_gather(quant, "col", axis=0, tiled=True),
        lax.all_gather(scale, "col", axis=0, tiled=True),
    )
    factor = scale_full.astype(jnp.float32)
    gate_out = lax.psum_scatter(
        jnp.dot(quant_full, gate_weight, preferred_element_type=jnp.float32) * factor[:, None],
        "row",
        scatter_dimension=0,
        tiled=True,
    )
    return (gate_out, token_peak)


def solution(mesh):
    in_specs = (P("col", "row"), P("row"), P("row", "col"))
    out_specs = (P("row", "col"), P("col"))
    return jax.shard_map(shards, mesh=mesh, in_specs=in_specs, out_specs=out_specs, check_vma=False)
```

profile of v0, /device:TPU:0, one launch (start us, length us, event | category | flops | bytes accessed | tf_op | source)
XLA Modules:
  0.0 409.6 jit_solution(14149842245059294709)
XLA Ops:
  7.2 0.0 all-gather.3.cloned.1.call-start
  7.2 0.7 convert_element_type.27
  7.9 1.3 fusion
  9.3 11.5 %all_to_all.5 = f32[16,2,256]{2,1,0:T(2,128)S(1)} all-to-all(f32[16,2,256]{2,1,0:T(2,128)S(1)} %broadcast_in_dim.2), channel_id=1, replica_groups=mesh['row'=16,'col'=8] {'row'}, dimensions={0} | all-to-all | bytes 65536 | tf_op jit(solution)/shard_map/all_to_all | solution.py:11
  21.1 0.6 fusion.7
  21.7 2.1 fusion.5
  23.7 0.0 all-gather.3.cloned.1.call-update
  23.8 0.0 reduce-scatter.2.cloned.1.call-start
  23.8 24.3 %all-gather = bf16[8,1,256]{2,1,0:T(2,128)(2,1)S(1)} all-gather(bf16[1,1,256]{2,1,0:T(2,128)(2,1)S(1)} %reshape.47), channel_id=1, replica_groups=mesh['row'=16,'col'=8] {'col'}, dimensions={0}, use_global_device_ids=true | all-gather | bytes 4608 | tf_op jit(solution)/shard_map/all_gather | solution.py:63
  48.2 47.1 %all-gather.3.cloned.1.call-done = bf16[2048,1024]{1,0:T(8,128)(2,1)} async-done(((bf16[256,1024]{1,0:T(8,128)(2,1)}), bf16[2048,1024]{1,0:T(8,128)(2,1)}) %all-gather.3.cloned.1.call-update) | async-done | bytes 4194320 | tf_op jit(solution)/shard_map/all_gather | solution.py:62
  95.3 21.6 %convolution_multiply_fusion = f32[2048,3328]{1,0:T(8,128)} fusion(bf16[2048,1024]{1,0:T(8,128)(2,1)} %all-gather.3.cloned.1.call-done, bf16[1024,3328]{1,0:T(8,128)(2,1)} %param.5, f32[2048]{0:T(1024)S(1)} %bitcast.13), kind=kOutput, calls=%fused_computation | convolution fusion | flops 13965459456 | bytes 38281216 | tf_op jit(solution)/shard_map/dot_general | solution.py:67
  116.9 0.0 reduce-scatter.2.cloned.1.call-update
  116.9 285.8 %reduce-scatter.2.cloned.1.call-done = f32[128,3328]{1,0:T(8,128)} async-done(((f32[2048,3328]{1,0:T(8,128)}), f32[128,3328]{1,0:T(8,128)}) %reduce-scatter.2.cloned.1.call-update) | async-done | bytes 1703952 | tf_op jit(solution)/shard_map/reduce_scatter | solution.py:66
  (26 shorter events, 0.4 us)
Async XLA Ops:
  7.2 88.1 %all-gather.3.cloned.1.call-start = ((), (), s32[]{:S(2)}) async-start(), calls=%async_computation.2 | async-start | bytes 4718592 | tf_op jit(solution)/shard_map/all_gather | solution.py:62
  23.8 379.0 %reduce-scatter.2.cloned.1.call-start = ((), (), s32[]{:S(2)}) async-start(), calls=%async_computation.3 | async-start | bytes 28966912 | tf_op jit(solution)/shard_map/reduce_scatter | solution.py:66
Sparse Core Ops, SparseCore 0:
  23.9 71.3 all-gather.2
  117.1 285.6 reduce-scatter.1
where the time goes:
time: 410 us
  waiting for transfers between devices  333 us (81%)
  blocking collectives  35.9 us (9%)
  matrix products  21.6 us (5%)
  between operations  14.1 us (3%)
  other arithmetic  4.7 us (1%)
    reduce_scatter x1, waiting for transfers between devices, shards(): lax.psum_scatter(jnp.dot(quant_full, gate_weight, preferred_element_type=...  286 us
    all_gather x1, waiting for transfers between devices, shards(): lax.all_gather(quant, 'col', axis=0, tiled=True)  47.1 us
    all_gather x1, blocking collectives, shards(): lax.all_gather(scale, 'col', axis=0, tiled=True)  24.3 us
    dot_general x1, matrix products, shards(): jnp.dot(quant_full, gate_weight, preferred_element_type=jnp.float32)  21.6 us
    all_to_all x1, blocking collectives, copy_for_each(): lax.all_to_all(jnp.broadcast_to(shard[None], (count, *shard.shape)), axis...  11.5 us
  transfers between devices with their start and end apart: 2, of which 2 were waited for; matrix products, arithmetic and copies ran while one was open for 0% of the time, Pallas kernels for 0%

commit v1 on v0

--- a/solution.py
+++ b/solution.py
@@ -59,7 +59,9 @@
     scale = ((token_peak + 1e-06) / 448.0).astype(jnp.bfloat16)
     quant = (normed / scale.astype(jnp.float32)[:, None]).astype(jnp.bfloat16)
     quant_full, scale_full = (
-        lax.all_gather(quant, "col", axis=0, tiled=True),
+        jnp.concatenate(
+            lax.all_to_all(jnp.stack([quant] * lax.axis_size("col")), "col", 0, 0), axis=0
+        ),
         lax.all_gather(scale, "col", axis=0, tiled=True),
     )
     factor = scale_full.astype(jnp.float32)

time: 410 us -> 409 us (level)
  waiting for transfers between devices: 333 us -> 285 us
  blocking collectives: 35.9 us -> 73.8 us
  starting transfers between devices: 0.08 us -> 7.52 us
    all_gather x1 -> x0, waiting for transfers between devices: 47.1 us -> none  [shards(): lax.all_gather(quant, 'col', axis=0, tiled=True)]
    all_gather x1, blocking collectives: 24.3 us -> 62.3 us  [shards(): lax.all_gather(scale, 'col', axis=0, tiled=True)]
    all_to_all x0 -> x1, starting transfers between devices: none -> 7.48 us  [shards(): lax.all_to_all(jnp.stack([quant] * lax.axis_size('col')), 'col', 0, 0)]
  transfers between devices with their start and end apart: 2 -> 2, of which waited for: 2 -> 1; matrix products, arithmetic and copies ran while one was open for 0% -> 0% of each run, Pallas kernels for 0% -> 0%
where the time goes in v1:
time: 409 us
  waiting for transfers between devices  285 us (70%)
  blocking collectives  73.8 us (18%)
  matrix products  21.6 us (5%)
  between operations  14.1 us (3%)
  starting transfers between devices  7.52 us (2%)
    reduce_scatter x1, waiting for transfers between devices, shards(): lax.psum_scatter(jnp.dot(quant_full, gate_weight, preferred_element_type=...  285 us
    all_gather x1, blocking collectives, shards(): lax.all_gather(scale, 'col', axis=0, tiled=True)  62.3 us
    dot_general x1, matrix products, shards(): jnp.dot(quant_full, gate_weight, preferred_element_type=jnp.float32)  21.6 us
    all_to_all x1, blocking collectives, copy_for_each(): lax.all_to_all(jnp.broadcast_to(shard[None], (count, *shard.shape)), axis...  11.5 us
  transfers between devices with their start and end apart: 2, of which 1 were waited for; matrix products, arithmetic and copies ran while one was open for 0% of the time, Pallas kernels for 0%

profile of v1, /device:TPU:0, one launch (start us, length us, event | category | flops | bytes accessed | tf_op | source)
XLA Modules:
  0.0 408.6 jit_solution(7321253781278059411)
XLA Ops:
  7.2 0.7 convert_element_type.27
  7.8 1.3 fusion
  9.2 11.5 %all_to_all.10 = f32[16,2,256]{2,1,0:T(2,128)S(1)} all-to-all(f32[16,2,256]{2,1,0:T(2,128)S(1)} %broadcast_in_dim.2), channel_id=1, replica_groups=mesh['row'=16,'col'=8] {'row'}, dimensions={0} | all-to-all | bytes 65536 | tf_op jit(solution)/shard_map/all_to_all | solution.py:11
  21.1 0.6 fusion.7
  21.6 1.3 fusion.5
  22.9 2.5 stack.2
  25.4 7.5 %all-to-all-start.1 = ((bf16[8,256,1024]{2,1,0:T(8,128)(2,1)}), bf16[8,256,1024]{2,1,0:T(8,128)(2,1)}, u32[]{:S(2)}, u32[]{:S(2)}) async-start(bf16[8,256,1024]{2,1,0:T(8,128)(2,1)} %stack.2), calls=%async_computation.1 | async-start | bytes 8388608 | tf_op jit(solution)/shard_map/all_to_all | solution.py:63
  32.9 0.0 reduce-scatter.2.cloned.1.call-start
  32.9 62.3 %all-gather = bf16[8,1,256]{2,1,0:T(2,128)(2,1)S(1)} all-gather(bf16[1,1,256]{2,1,0:T(2,128)(2,1)S(1)} %reshape.53), channel_id=1, replica_groups=mesh['row'=16,'col'=8] {'col'}, dimensions={0}, use_global_device_ids=true | all-gather | bytes 4608 | tf_op jit(solution)/shard_map/all_gather | solution.py:65
  95.2 0.0 all-to-all-done.1
  95.2 21.6 %convolution_multiply_fusion = f32[2048,3328]{1,0:T(8,128)} fusion(bf16[2048,1024]{1,0:T(8,128)(2,1)} %bitcast.4, bf16[1024,3328]{1,0:T(8,128)(2,1)} %param.5, f32[2048]{0:T(1024)S(1)} %bitcast.14), kind=kOutput, calls=%fused_computation | convolution fusion | flops 13965459456 | bytes 38281216 | tf_op jit(solution)/shard_map/dot_general | solution.py:69
  116.9 0.0 reduce-scatter.2.cloned.1.call-update
  116.9 284.8 %reduce-scatter.2.cloned.1.call-done = f32[128,3328]{1,0:T(8,128)} async-done(((f32[2048,3328]{1,0:T(8,128)}), f32[128,3328]{1,0:T(8,128)}) %reduce-scatter.2.cloned.1.call-update) | async-done | bytes 1703952 | tf_op jit(solution)/shard_map/reduce_scatter | solution.py:68
  (26 shorter events, 0.4 us)
Async XLA Ops:
  25.4 69.8 %all-to-all-start.1 = ((bf16[8,256,1024]{2,1,0:T(8,128)(2,1)}), bf16[8,256,1024]{2,1,0:T(8,128)(2,1)}, u32[]{:S(2)}, u32[]{:S(2)}) async-start(bf16[8,256,1024]{2,1,0:T(8,128)(2,1)} %stack.2), calls=%async_computation.1 | async-start | bytes 8388608 | tf_op jit(solution)/shard_map/all_to_all | solution.py:63
  32.9 368.9 %reduce-scatter.2.cloned.1.call-start = ((), (), s32[]{:S(2)}) async-start(), calls=%async_computation.3 | async-start | bytes 28966912 | tf_op jit(solution)/shard_map/reduce_scatter | solution.py:68
Sparse Core Ops, SparseCore 0:
  117.0 284.6 reduce-scatter.1
